TPU v7x, 32 devices: a whole 2x2x4 slice. The times are simulated.
32 devices in a mesh: group: 2 (over y), chan: 4 (over z), band: 2 (over x), beam: 2 (over core).
Axes of the slice: x: 2, y: 2, z: 4, core: 2. Of those that a mesh axis runs over, the one named last changes fastest.
Arguments:
- voltages: bfloat16 [2, 1024, 2, 8, 512], P(None, 'chan', 'band', None, 'group'), parts along dimension 4, may hold values from -6 to 6
- gains: float32 [2, 2, 8, 1024], P(None, 'band', 'chan'), may hold values from -5 to 5
- positions: float32 [3, 1024], replicated, may hold values from -4 to 4
- directions: float32 [3, 2048], P(None, ('group', 'beam')), parts along dimension 1, may hold values from -1 to 1
- antenna_row_lookup: int32 [1024], replicated, may hold values from 0 to 1023, each once
- chan_order: int32 [16], replicated, may hold values from 0 to 15, each once
- delays: int32 [4, 2, 8], replicated, may hold values from 0 to 31
Outputs:
- dedispersed: float32 [2, 8, 32, 2048], P('band', 'chan', None, ('group', 'beam')), parts along dimension 3
There are 2 independent parts, one for each index of `group`. A program takes and returns all parts, laid end to end along the dimension named above; an argument that names none is the same for every part. Nothing has to cross between parts.
Inputs may be any that keep to these rules, and one draw needn't show every extreme that they name: `antenna_row_lookup`: each antenna appears once. `chan_order`: each frequency index appears once.
All inputs are finite; a program needn't handle non-finite values.
Results may differ from a plain program's by a relative error of at most 0.004.
Values may be sent and summed in bfloat16 or wider, within the bound.
A program may use at most 64 MiB of HBM per device.

v0:
```python
import math

import jax
import jax.numpy as jnp
from jax import lax
from jax.sharding import PartitionSpec as P

INTEG = 8


def partner_2(value, axis, distance):
    mask = 2**distance
    pairs = [(source, source ^ mask) for source in range(lax.axis_size(axis))]
    return lax.ppermute(value, axis, pairs)


def roll_rows(state, shifts):
    length = state.shape[1]
    doubled = jnp.concatenate([state, state], axis=1)

    def one_row(row, shift):
        return lax.dynamic_slice_in_dim(row, length - shift, length, 0)

    return jax.vmap(one_row)(doubled, shifts)


def pair_round(state, shifts, stride):
    count, length, width = state.shape
    grouped = state.reshape(count // (2 * stride), 2, stride, length, width)
    lower = jnp.broadcast_to(grouped[:, 0:1], grouped.shape).reshape(state.shape)
    upper = jnp.broadcast_to(grouped[:, 1:2], grouped.shape).reshape(state.shape)
    return lower + roll_rows(upper, shifts)


def partner_round(state, partner, upper_side, shifts):
    lower = jnp.where(upper_side, partner, state)
    upper = jnp.where(upper_side, state, partner)
    return lower + roll_rows(upper, shifts)


def beam_weights(gain_pair, freq, pos_rows, dirs):
    geometry = pos_rows[0][:, None] * dirs[0][None, :]
    geometry = geometry + pos_rows[1][:, None] * dirs[1][None, :]
    geometry = geometry + pos_rows[2][:, None] * dirs[2][None, :]
    phase = (2.0 * math.pi * freq)[:, None, None] * geometry[None]
    cosine = jnp.cos(phase)
    sine = jnp.sin(phase)
    g_re = gain_pair[0][:, :, None]
    g_im = gain_pair[1][:, :, None]
    factor = 1.0 / math.sqrt(pos_rows.shape[1])
    w_re = ((g_re * cosine + g_im * sine) * factor).astype(jnp.bfloat16)
    w_im = ((g_im * cosine - g_re * sine) * factor).astype(jnp.bfloat16)
    upper_rows = jnp.concatenate([w_re, w_im], axis=2)
    lower_rows = jnp.concatenate([-w_im, w_re], axis=2)
    return jnp.stack([upper_rows, lower_rows], axis=1)


def integrate(power, chans):
    count, samples, width = power.shape
    binned = jnp.mean(power.reshape(count, samples // INTEG, INTEG, width), axis=2)
    centred = binned - jnp.mean(binned, axis=1, keepdims=True)
    return centred * (1.0 / math.sqrt(chans))


def shards(voltages, gains, positions, directions, antenna_row_lookup, chan_order, delays):
    chan_count = lax.axis_size("chan")
    band_count = lax.axis_size("band")
    per_dev = gains.shape[2]
    in_band = per_dev * chan_count
    total = in_band * band_count
    chan_index = lax.axis_index("chan")
    band_index = lax.axis_index("band")
    base = band_index * in_band + chan_index * per_dev
    freq = 1.0 + lax.dynamic_slice_in_dim(chan_order, base, per_dev).astype(jnp.float32) / total
    pos_rows = positions[:, antenna_row_lookup]
    weights = beam_weights(gains[:, 0], freq, pos_rows, directions)
    turned = lax.all_to_all(voltages, "chan", split_axis=3, concat_axis=1, tiled=True)
    flat = turned.reshape(turned.shape[0], turned.shape[1], turned.shape[3], turned.shape[4])
    beams = jnp.einsum("pacn,cpaq->cnq", flat, weights, preferred_element_type=jnp.float32)
    half = beams.shape[2] // 2
    power = beams[:, :, :half] * beams[:, :, :half] + beams[:, :, half:] * beams[:, :, half:]
    state = integrate(power, total)
    flat_delays = delays.reshape(delays.shape[0], total)
    local_bits = per_dev.bit_length() - 1
    chan_bits = chan_count.bit_length() - 1
    band_bits = band_count.bit_length() - 1
    bit = 0
    shifts = lax.dynamic_slice_in_dim(flat_delays[bit], base, per_dev)
    state = pair_round(state, shifts, 1 << bit)
    for bit in range(chan_bits):
        level_no = local_bits + bit
        shifts = lax.dynamic_slice_in_dim(flat_delays[level_no], base, per_dev)
        partner = partner_2(state, "chan", bit)
        upper_side = chan_index // (1 << bit) % 2 == 1
        state = partner_round(state, partner, upper_side, shifts)
    for bit in range(band_bits):
        level_no = local_bits + chan_bits + bit
        shifts = lax.dynamic_slice_in_dim(flat_delays[level_no], base, per_dev)
        partner = partner_2(state, "band", bit)
        upper_side = band_index // (1 << bit) % 2 == 1
        state = partner_round(state, partner, upper_side, shifts)
    return state.reshape(1, per_dev, state.shape[1], state.shape[2])


def solution(mesh):
    placed = (
        P(None, "chan", "band", None, "group"),
        P(None, "band", "chan", None),
        P(),
        P(None, ("group", "beam")),
        P(),
        P(),
        P(),
    )
    return jax.shard_map(
        shards,
        mesh=mesh,
        in_specs=placed,
        out_specs=P("band", "chan", None, ("group", "beam")),
        check_vma=False,
    )
```

profile of v0, /device:TPU:0, one launch (start us, length us, event | category | flops | bytes accessed | tf_op | source)
XLA Modules:
  0.0 94.2 jit_solution(8014257760844754673)
XLA Ops:
  0.0 3.5 %copy.29 = bf16[2,256,1,8,256]{4,1,2,0,3:T(8,128)(2,1)} copy(bf16[2,256,1,8,256]{4,3,2,1,0:T(8,128)(2,1)} %param.7) | data formatting | bytes 4194304 | tf_op args[0]
  3.5 6.4 %all-to-all-start = ((bf16[2,256,1,8,256]{4,1,2,0,3:T(8,128)(2,1)}), bf16[2,256,1,8,256]{4,1,2,0,3:T(8,128)(2,1)S(1)}, u32[]{:S(2)}, u32[]{:S(2)}) async-start(bf16[2,256,1,8,256]{4,1,2,0,3:T(8,128)(2,1)} %copy.29), calls=%async_computation | async-start | bytes 4194304 | tf_op jit(solution)/shard_map/all_to_all | solution.py:77
  9.9 0.0 copy-done
  9.9 0.2 copy.27
  10.2 0.1 squeeze.13
  10.3 0.0 copy-done.4
  10.3 2.8 %gather_fusion = f32[1024,3]{1,0:T(8,128)S(1)} fusion(f32[3,1024]{0,1:T(8,128)S(1)} %copy.27, s32[1024]{0:T(1024)S(1)} %fusion.21), kind=kCustom, calls=%fused_computation | custom fusion | bytes 28672 | tf_op jit(solution)/shard_map/gather | solution.py:75
  13.1 0.0 copy-done.5
  13.1 0.1 add_multiply_fusion
  13.2 0.1 fusion.29
  13.3 0.8 slice_reduce_fusion.2
  14.0 0.0 copy-done.2
  14.1 0.0 copy-done.1
  14.1 0.5 multiply_add_fusion
  14.6 15.9 %fusion.10 = bf16[2,1024,512]{2,1,0:T(8,128)(2,1)S(1)} fusion(f32[2,1024]{1,0:T(2,128)S(1)} %get-tuple-element.15, f32[1024,512]{1,0:T(8,128)S(1)} %multiply_add_fusion, f32[2]{0:T(128)S(1)} %add_multiply_fusion, f32[2,1024]{1,0:T(2,128)S(1)} %get-tuple-element.14), kind=kLoop, calls=%fused_computation.17 | loop fusion | flops 6291456 | bytes 4210696 | tf_op jit(solution)/shard_map/convert_element_type | solution.py:51
  30.4 16.1 %fusion.31 = (bf16[2,1024,512]{2,1,0:T(8,128)(2,1)S(1)}, bf16[2,1024,512]{2,1,0:T(8,128)(2,1)S(1)}) fusion(f32[2,1024]{1,0:T(2,128)S(1)} %get-tuple-element.14, f32[1024,512]{1,0:T(8,128)S(1)} %multiply_add_fusion, f32[2]{0:T(128)S(1)} %add_multiply_fusion, f32[2,1024]{1,0:T(2,128)S(1)} %get-tuple-element.15), kind=kLoop, calls=%fused_computation.73 | loop fusion | flops 9437184 | bytes 6307848 | tf_op jit(solution)/shard_map/neg | solution.py:54
  46.6 3.9 %maximum_bitcast_fusion = (bf16[2,1,1024,1024]{3,2,1,0:T(8,128)(2,1)}, bf16[2,1,1024,1024]{3,2,1,0:T(8,128)(2,1)}) fusion(bf16[2,1024,512]{2,1,0:T(8,128)(2,1)S(1)} %get-tuple-element.9, bf16[2,1024,512]{2,1,0:T(8,128)(2,1)S(1)} %fusion.10, bf16[2,1024,512]{2,1,0:T(8,128)(2,1)S(1)} %get-tuple-element.8), kind=kLoop, calls=%fused_computation.21 | loop fusion | flops 16777216 | bytes 14680064 | tf_op jit(solution)/shard_map/stack | solution.py:55
  50.5 7.6 %all-to-all-done = bf16[2,256,1,8,256]{4,1,2,0,3:T(8,128)(2,1)S(1)} async-done(((bf16[2,256,1,8,256]{4,1,2,0,3:T(8,128)(2,1)}), bf16[2,256,1,8,256]{4,1,2,0,3:T(8,128)(2,1)S(1)}, u32[]{:S(2)}, u32[]{:S(2)}) %all-to-all-start) | async-done | bytes 2097184 | tf_op jit(solution)/shard_map/all_to_all | solution.py:77
  58.1 1.5 %copy.30 = bf16[2,256,1,8,256]{4,1,3,0,2:T(8,128)(2,1)} copy(bf16[2,256,1,8,256]{4,1,2,0,3:T(8,128)(2,1)S(1)} %all-to-all-done) | data formatting | bytes 4194304 | tf_op jit(solution)/shard_map/all_to_all | solution.py:77
  59.6 3.1 %copy.31 = bf16[2,4,256,1,2,256]{2,1,5,0,4,3:T(4,128)(2,1)S(1)} copy(bf16[2,4,256,1,2,256]{5,2,4,1,0,3:T(8,128)(2,1)} %bitcast.73) | data formatting | bytes 4194304 | tf_op jit(solution)/shard_map/all_to_all | solution.py:77
  62.7 2.7 %reshape.148 = bf16[2,1024,2,256]{1,3,0,2:T(8,128)(2,1)} reshape(bf16[2,4,256,1,2,256]{2,1,5,0,4,3:T(4,128)(2,1)S(1)} %copy.31) | data formatting | bytes 4194304 | tf_op jit(solution)/shard_map/reshape | solution.py:78
  65.4 5.4 %fusion.14 = f32[2,256,1024]{2,1,0:T(8,128)S(1)} fusion(bf16[2,1024,2,256]{1,3,0,2:T(8,128)(2,1)} %reshape.148, bf16[2,1,1024,1024]{3,2,1,0:T(8,128)(2,1)} %get-tuple-element.11, bf16[2,1,1024,1024]{3,2,1,0:T(8,128)(2,1)} %get-tuple-element.10), kind=kOutput, calls=%fused_computation.24 | convolution fusion | flops 2164260864 | bytes 12582912 | tf_op jit(solution)/shard_map/pacn,cpaq->cnq/dot_general | solution.py:79
  70.9 0.5 fusion.19
  71.5 0.1 pad_maximum_fusion
  71.6 1.1 %gather_fusion.1 = f32[2,32,512]{2,0,1:T(2,128)S(1)} fusion(f32[2,64,512]{2,0,1:T(2,128)S(1)} %pad_maximum_fusion, s32[2]{0:T(128)S(1)} %fusion.29), kind=kCustom, calls=%fused_computation.1 | custom fusion | bytes 262168 | tf_op jit(solution)/shard_map/vmap()/gather | solution.py:22
  72.7 0.1 broadcast_add_fusion
  72.8 0.1 collective-permute-start
  72.8 0.1 squeeze.14
  72.9 0.1 fusion.28
  73.0 4.8 %collective-permute-done = f32[2,32,512]{2,0,1:T(2,128)S(1)} collective-permute-done((f32[2,32,512]{2,0,1:T(2,128)S(1)}, f32[2,32,512]{2,0,1:T(2,128)S(1)}, u32[]{:S(2)}, u32[]{:S(2)}) %collective-permute-start) | collective-permute-done | bytes 131104 | tf_op jit(solution)/shard_map/ppermute | solution.py:14
  77.8 0.1 broadcast_select_fusion
  77.9 0.1 pad_maximum_fusion.1
  78.0 1.1 %gather_fusion.2 = f32[2,32,512]{2,0,1:T(2,128)S(1)} fusion(f32[2,64,512]{2,0,1:T(2,128)S(1)} %pad_maximum_fusion.1, s32[2]{0:T(128)S(1)} %fusion.28), kind=kCustom, calls=%fused_computation.2 | custom fusion | bytes 262168 | tf_op jit(solution)/shard_map/vmap()/gather | solution.py:22
  79.1 0.1 select_add_fusion.1
  79.2 0.1 collective-permute-start.1
  79.3 0.1 squeeze.15
  79.4 0.1 fusion.27
  79.5 6.5 %collective-permute-done.1 = f32[2,32,512]{2,0,1:T(2,128)S(1)} collective-permute-done((f32[2,32,512]{2,0,1:T(2,128)S(1)}, f32[2,32,512]{2,0,1:T(2,128)S(1)}, u32[]{:S(2)}, u32[]{:S(2)}) %collective-permute-start.1) | collective-permute-done | bytes 131104 | tf_op jit(solution)/shard_map/ppermute | solution.py:14
  86.0 0.1 pad_maximum_fusion.2
  86.1 1.1 %gather_fusion.3 = f32[2,32,512]{2,0,1:T(2,128)S(1)} fusion(f32[2,64,512]{2,0,1:T(2,128)S(1)} %pad_maximum_fusion.2, s32[2]{0:T(128)S(1)} %fusion.27), kind=kCustom, calls=%fused_computation.3 | custom fusion | bytes 262168 | tf_op jit(solution)/shard_map/vmap()/gather | solution.py:22
  87.2 1.6 %collective-permute-start.2 = (f32[2,32,512]{2,0,1:T(2,128)S(1)}, f32[2,32,512]{2,0,1:T(2,128)S(1)}, u32[]{:S(2)}, u32[]{:S(2)}) collective-permute-start(f32[2,32,512]{2,0,1:T(2,128)S(1)} %bitcast.75), channel_id=1, source_target_pairs={{0,2},{2,0},{1,3},{3,1},{4,6},{6,4},{5,7},{7,5},{8,10},{10,8},{9,1... | collective-permute-start | bytes 393224 | tf_op jit(solution)/shard_map/ppermute | solution.py:14
  88.8 0.1 squeeze.16
  88.9 0.1 fusion.26
  88.9 3.3 %collective-permute-done.2 = f32[2,32,512]{2,0,1:T(2,128)S(1)} collective-permute-done((f32[2,32,512]{2,0,1:T(2,128)S(1)}, f32[2,32,512]{2,0,1:T(2,128)S(1)}, u32[]{:S(2)}, u32[]{:S(2)}) %collective-permute-start.2) | collective-permute-done | bytes 131104 | tf_op jit(solution)/shard_map/ppermute | solution.py:14
  92.3 0.1 pad_maximum_fusion.3
  92.4 1.1 %gather_fusion.4 = f32[2,32,512]{2,0,1:T(2,128)S(1)} fusion(f32[2,64,512]{2,0,1:T(2,128)S(1)} %pad_maximum_fusion.3, s32[2]{0:T(128)S(1)} %fusion.26), kind=kCustom, calls=%fused_computation.4 | custom fusion | bytes 262168 | tf_op jit(solution)/shard_map/vmap()/gather | solution.py:22
  93.4 0.1 add_bitcast_fusion
  93.5 0.7 copy.32
  (19 shorter events, 0.2 us)
Async XLA Ops:
  0.0 9.9 %copy-start = (f32[3,1024]{1,0:T(4,128)S(1)}, f32[3,1024]{1,0:T(4,128)}, u32[]{:S(2)}) copy-start(f32[3,1024]{1,0:T(4,128)} %param.9) | copy-start | bytes 36868
  0.0 10.2 %copy-start.3 = (s32[4,2,8]{2,1,0:T(2,128)S(1)}, s32[4,2,8]{2,1,0:T(2,128)}, u32[]{:S(2)}) copy-start(s32[4,2,8]{2,1,0:T(2,128)} %param.13) | copy-start | bytes 772
  0.0 10.3 %copy-start.4 = (s32[1024]{0:T(1024)S(1)}, s32[1024]{0:T(1024)}, u32[]{:S(2)}) copy-start(s32[1024]{0:T(1024)} %param.11) | copy-start | bytes 12292
  0.0 13.1 %copy-start.5 = (s32[16]{0:T(128)S(1)}, s32[16]{0:T(128)}, u32[]{:S(2)}) copy-start(s32[16]{0:T(128)} %param.12) | copy-start | bytes 196
  3.5 10.6 %copy-start.2 = (f32[3,512]{1,0:T(4,128)S(1)}, f32[3,512]{1,0:T(4,128)}, u32[]{:S(2)}) copy-start(f32[3,512]{1,0:T(4,128)} %param.10) | copy-start | bytes 18436
  3.5 10.6 %copy-start.1 = (f32[2,1,2,1024]{3,2,1,0:T(2,128)S(1)}, f32[2,1,2,1024]{3,2,1,0:T(2,128)}, u32[]{:S(2)}) copy-start(f32[2,1,2,1024]{3,2,1,0:T(2,128)} %param.8) | copy-start | bytes 49156
  3.5 54.6 %all-to-all-start = ((bf16[2,256,1,8,256]{4,1,2,0,3:T(8,128)(2,1)}), bf16[2,256,1,8,256]{4,1,2,0,3:T(8,128)(2,1)S(1)}, u32[]{:S(2)}, u32[]{:S(2)}) async-start(bf16[2,256,1,8,256]{4,1,2,0,3:T(8,128)(2,1)} %copy.29), calls=%async_computation | async-start | bytes 4194304 | tf_op jit(solution)/shard_map/all_to_all | solution.py:77
  72.8 5.0 %collective-permute-start = (f32[2,32,512]{2,0,1:T(2,128)S(1)}, f32[2,32,512]{2,0,1:T(2,128)S(1)}, u32[]{:S(2)}, u32[]{:S(2)}) collective-permute-start(f32[2,32,512]{2,0,1:T(2,128)S(1)} %broadcast_add_fusion), channel_id=1, source_target_pairs={{0,4},{4,0},{8,12},{12,8},{1,5},{5,1},{9,13},{13,9},{2,6},{6,2},{1... | collective-permute-start | bytes 393224 | tf_op jit(solution)/shard_map/ppermute | solution.py:14
  79.2 6.8 %collective-permute-start.1 = (f32[2,32,512]{2,0,1:T(2,128)S(1)}, f32[2,32,512]{2,0,1:T(2,128)S(1)}, u32[]{:S(2)}, u32[]{:S(2)}) collective-permute-start(f32[2,32,512]{2,0,1:T(2,128)S(1)} %select_add_fusion.1), channel_id=1, source_target_pairs={{0,8},{4,12},{8,0},{12,4},{1,9},{5,13},{9,1},{13,5},{2,10},{6,14},... | collective-permute-start | bytes 393224 | tf_op jit(solution)/shard_map/ppermute | solution.py:14
  87.2 5.0 %collective-permute-start.2 = (f32[2,32,512]{2,0,1:T(2,128)S(1)}, f32[2,32,512]{2,0,1:T(2,128)S(1)}, u32[]{:S(2)}, u32[]{:S(2)}) collective-permute-start(f32[2,32,512]{2,0,1:T(2,128)S(1)} %bitcast.75), channel_id=1, source_target_pairs={{0,2},{2,0},{1,3},{3,1},{4,6},{6,4},{5,7},{7,5},{8,10},{10,8},{9,1... | collective-permute-start | bytes 393224 | tf_op jit(solution)/shard_map/ppermute | solution.py:14
where the time goes:
time: 94.5 us; the launch traced here: 94.2 us
  other arithmetic  38.1 us (40%)
  waiting for transfers between devices  22.3 us (24%)
  local copies, waits for them, and re-layouts  20 us (21%)
  starting transfers between devices  8.15 us (9%)
  matrix products  5.44 us (6%)
    neg x1, other arithmetic, beam_weights(): lower_rows = jnp.concatenate([-w_im, w_re], axis=2)  16.1 us
    convert_element_type x1, other arithmetic, beam_weights(): w_re = ((g_re * cosine + g_im * sine) * factor).astype(jnp.bfloat16)  15.9 us
    ppermute x3, waiting for transfers between devices, partner_2(): return lax.ppermute(value, axis, pairs)  14.6 us
    all_to_all x1, waiting for transfers between devices, shards(): lax.all_to_all(voltages, 'chan', split_axis=3, concat_axis=1, tiled=True)  7.65 us
    all_to_all x1, starting transfers between devices, shards(): lax.all_to_all(voltages, 'chan', split_axis=3, concat_axis=1, tiled=True)  6.45 us
    dot_general x1, matrix products, shards(): jnp.einsum('pacn,cpaq->cnq', flat, weights, preferred_element_type=jnp.fl...  5.44 us
    all_to_all x2, local copies, waits for them, and re-layouts, shards(): lax.all_to_all(voltages, 'chan', split_axis=3, concat_axis=1, tiled=True)  4.56 us
    gather x4, local copies, waits for them, and re-layouts, one_row(): return lax.dynamic_slice_in_dim(row, length - shift, length, 0)  4.3 us
  transfers between devices with their start and end apart: 4, of which 4 were waited for; matrix products, arithmetic and copies ran while one was open for 43% of the time, Pallas kernels for 0%

commit v1 on v0

v1 whole, which is shorter than its diff:
```python
import functools
import math

import jax
import jax.numpy as jnp
from jax import lax
from jax.experimental import pallas as pl
from jax.experimental.pallas import tpu as pltpu
from jax.sharding import PartitionSpec as P

INTEG = 8
MESH = pl.DeviceIdType.MESH
SIN = (4.44288283, -7.30824114, 3.60628867, -0.84576206, 0.10920298)
COS = (1.4142135, -6.97885095, 5.73946031, -1.88355744, 0.31068696)
CUTS = 2


def horner(coefs, x):
    total = jnp.full_like(x, coefs[-1])
    for coef in coefs[-2::-1]:
        total = total * x + coef
    return total


def roll_down(state, shift):
    rows = state.shape[0]
    for bit in range(rows.bit_length() - 1):
        moved = pltpu.roll(state, 1 << bit, 0)
        state = jnp.where((shift >> bit) & 1 == 1, moved, state)
    return state


def kernel(
    zs, bands, total, order_ref, delay_ref, volt_ref, gain_ref, pos_ref, dirs_ref, lookup_ref, out_ref,
    send, recv, table, weights, acc, other_dirs, level, other_level, tx, rx, select,
    v_send, v_recv, d_send, d_recv, l_send, l_recv, t_send, t_recv,
):
    z = lax.axis_index("chan")
    x = lax.axis_index("band")
    core = lax.axis_index("beam")
    antennas = lookup_ref.shape[1]
    local_ants = antennas // zs
    in_band = 2 * zs
    half = dirs_ref.shape[1]
    bins = level.shape[1]
    z_bits = zs.bit_length() - 1
    x_bits = bands.bit_length() - 1
    slot = x * in_band + z * 2 + core

    barrier = pltpu.get_barrier_semaphore()
    for d in range(1, zs):
        pl.semaphore_signal(barrier, inc=1, device_id={"chan": (z + d) % zs}, device_id_type=MESH)
    pl.semaphore_signal(barrier, inc=1, device_id={"beam": 1 - core}, device_id_type=MESH)
    for bit in range(x_bits):
        pl.semaphore_signal(barrier, inc=1, device_id={"band": x ^ (1 << bit)}, device_id_type=MESH)

    ants = select.shape[0] // zs
    rows = lax.broadcasted_iota(jnp.int32, select.shape, 0)
    cols = lax.broadcasted_iota(jnp.int32, select.shape, 1)
    ant_bits = ants.bit_length() - 1
    wanted = (rows & (ants - 1)) * in_band + (rows >> ant_bits) * 2 + core
    select[...] = jnp.where(cols == wanted, 1.0, 0.0).astype(jnp.bfloat16)
    for part in range(2):
        for block in range(local_ants // ants):
            lines = volt_ref[part, block * ants * in_band : (block + 1) * ants * in_band, :]
            picked = jnp.dot(select[...], lines, preferred_element_type=jnp.float32).astype(jnp.bfloat16)
            start = part * local_ants + block * ants
            for dest in range(zs):
                send[dest, start : start + ants, :] = picked[dest * ants : (dest + 1) * ants]

    pl.semaphore_wait(barrier, zs + x_bits)
    copies = []
    for d in range(1, zs):
        dest = (z + d) % zs
        copy = pltpu.make_async_remote_copy(
            src_ref=send.at[dest], dst_ref=recv.at[d - 1], send_sem=v_send.at[d - 1], recv_sem=v_recv.at[d - 1],
            device_id={"chan": dest}, device_id_type=MESH,
        )
        copy.start()
        copies.append(copy)
    dirs_copy = pltpu.make_async_remote_copy(
        src_ref=dirs_ref, dst_ref=other_dirs, send_sem=d_send, recv_sem=d_recv,
        device_id={"beam": 1 - core}, device_id_type=MESH,
    )
    dirs_copy.start()

    freq = 1.0 + order_ref[slot].astype(jnp.float32) / total
    pos = pos_ref[...]
    top = pos.astype(jnp.bfloat16)
    rest = pos - top.astype(jnp.float32)
    middle = rest.astype(jnp.bfloat16)
    last = (rest - middle.astype(jnp.float32)).astype(jnp.bfloat16)
    wide = 256
    for block in range(antennas // wide):
        span = slice(block * wide, (block + 1) * wide)
        row_no = lax.broadcasted_iota(jnp.int32, (antennas, wide), 0)
        hot = jnp.where(row_no == lookup_ref[:, span], 1.0, 0.0).astype(jnp.bfloat16)
        gathered = jnp.dot(top, hot, preferred_element_type=jnp.float32)
        gathered = gathered + jnp.dot(middle, hot, preferred_element_type=jnp.float32)
        gathered = gathered + jnp.dot(last, hot, preferred_element_type=jnp.float32)
        lines = gathered * freq + gain_ref[:, span] * (1.0 / math.sqrt(antennas))
        table[span, :] = lines.T

    tile = 16

    def fill(side, dirs):
        def step(index, carry):
            d = index // (local_ants // tile)
            row = (index % (local_ants // tile)) * tile
            source = (z - d + zs) % zs
            info = table[pl.ds(pl.multiple_of(source * local_ants + row, tile), tile), :]
            turns = info[:, 0:1] * dirs[0:1, :] + info[:, 1:2] * dirs[1:2, :] + info[:, 2:3] * dirs[2:3, :]
            r = turns - lax.round(turns, lax.RoundingMethod.TO_NEAREST_EVEN)
            sq = r * r
            s = r * horner(SIN, sq)
            c = horner(COS, sq)
            sine = s * c
            cosine = 1.0 - s * s
            g_re, g_im = info[:, 3:4], info[:, 4:5]
            w_re = (g_re * cosine + g_im * sine).astype(jnp.bfloat16)
            w_im = (g_im * cosine - g_re * sine).astype(jnp.bfloat16)
            columns = slice(side * half, (side + 1) * half)
            at = pl.multiple_of(row, tile)
            weights[d, pl.ds(at, tile), columns] = w_im
            weights[d, pl.ds(local_ants + at, tile), columns] = w_re
            weights[d, pl.ds(2 * local_ants + at, tile), columns] = -w_im
            return carry

        lax.fori_loop(0, antennas // tile, step, 0)

    fill(0, dirs_ref)
    dirs_copy.wait()
    fill(1, other_dirs)

    contract = (((0,), (0,)), ((), ()))
    for d in range(zs):
        if d == 0:
            block = send[z]
        else:
            copies[d - 1].wait()
            block = recv[d - 1]
        re = lax.dot_general(
            block, weights[d, local_ants : 3 * local_ants, :], contract, preferred_element_type=jnp.float32
        )
        im = lax.dot_general(
            block, weights[d, : 2 * local_ants, :], contract, preferred_element_type=jnp.float32
        )
        if d == 0:
            acc[0], acc[1] = re, im
        elif d < zs - 1:
            acc[0] += re
            acc[1] += im
        else:
            re = acc[0] + re
            im = acc[1] + im
    power = re * re + im * im
    binned = jnp.mean(power.reshape(bins, INTEG, 2 * half), axis=1)
    centred = (binned - jnp.mean(binned, axis=0, keepdims=True)) * (1.0 / math.sqrt(total))
    level[0] = centred[:, :half]
    level[1] = centred[:, half:]

    swap = pltpu.make_async_remote_copy(
        src_ref=level.at[1], dst_ref=other_level, send_sem=l_send, recv_sem=l_recv,
        device_id={"beam": 1 - core}, device_id_type=MESH,
    )
    swap.start()
    swap.wait()
    base = x * in_band + z * 2
    width = half // CUTS
    rounds = [("chan", bit) for bit in range(z_bits)] + [("band", bit) for bit in range(x_bits)]

    def send_round(no, cut, states):
        axis, bit = rounds[no]
        for ch in range(2):
            tx[no, cut, ch] = states[ch].astype(jnp.bfloat16)
        copy = pltpu.make_async_remote_copy(
            src_ref=tx.at[no, cut], dst_ref=rx.at[no, cut], send_sem=t_send.at[no, cut], recv_sem=t_recv.at[no, cut],
            device_id={axis: (z if axis == "chan" else x) ^ (1 << bit)}, device_id_type=MESH,
        )
        copy.start()
        return copy

    held, flights = [], []
    for cut in range(CUTS):
        span = slice(cut * width, (cut + 1) * width)
        mine, theirs = level[0, :, span], other_level[:, span]
        lower = jnp.where(core == 0, mine, theirs)
        upper = jnp.where(core == 0, theirs, mine)
        states = [lower + roll_down(upper, delay_ref[0, base + ch]) for ch in range(2)]
        held.append(states)
        flights.append(send_round(0, cut, states))
    for no, (axis, bit) in enumerate(rounds):
        place = z if axis == "chan" else x
        is_upper = (place >> bit) & 1 == 1
        for cut in range(CUTS):
            flights[cut].wait()
            states = []
            for ch in range(2):
                mine, theirs = held[cut][ch], rx[no, cut, ch].astype(jnp.float32)
                lower = jnp.where(is_upper, theirs, mine)
                upper = jnp.where(is_upper, mine, theirs)
                states.append(lower + roll_down(upper, delay_ref[no + 1, base + ch]))
            held[cut] = states
            if no + 1 < len(rounds):
                flights[cut] = send_round(no + 1, cut, states)
            else:
                for ch in range(2):
                    out_ref[ch, :, cut * width : (cut + 1) * width] = states[ch]


def shards(voltages, gains, positions, directions, antenna_row_lookup, chan_order, delays):
    zs = lax.axis_size("chan")
    bands = lax.axis_size("band")
    in_band = voltages.shape[3]
    total = in_band * bands
    antennas = positions.shape[1]
    local_ants = voltages.shape[1]
    samples = voltages.shape[4]
    bins = samples // INTEG
    half = directions.shape[1]
    ants = max(16, 256 // in_band)
    rounds = delays.shape[0]
    steps = rounds - 1
    core = lax.axis_index("beam")
    lines = voltages.reshape(2, local_ants * in_band, samples)
    gain = lax.dynamic_index_in_dim(gains[:, 0], core, 1, keepdims=False)
    gain = jnp.pad(gain, ((3, 3), (0, 0)))
    pos = jnp.pad(positions, ((0, 5), (0, 0)))
    dma = pltpu.SemaphoreType.DMA
    smem = pl.BlockSpec(memory_space=pltpu.SMEM)
    vmem = pl.BlockSpec(memory_space=pltpu.VMEM)
    out = pl.pallas_call(
        functools.partial(kernel, zs, bands, total),
        out_shape=jax.ShapeDtypeStruct((2, bins, half), jnp.float32),
        in_specs=[smem, smem, vmem, vmem, vmem, vmem, vmem],
        out_specs=vmem,
        scratch_shapes=[
            pltpu.VMEM((zs, 2 * local_ants, samples), jnp.bfloat16),
            pltpu.VMEM((zs - 1, 2 * local_ants, samples), jnp.bfloat16),
            pltpu.VMEM((antennas, 8), jnp.float32),
            pltpu.VMEM((zs, 3 * local_ants, 2 * half), jnp.bfloat16),
            pltpu.VMEM((2, samples, 2 * half), jnp.float32),
            pltpu.VMEM(directions.shape, jnp.float32),
            pltpu.VMEM((2, bins, half), jnp.float32),
            pltpu.VMEM((bins, half), jnp.float32),
            pltpu.VMEM((steps, CUTS, 2, bins, half // CUTS), jnp.bfloat16),
            pltpu.VMEM((steps, CUTS, 2, bins, half // CUTS), jnp.bfloat16),
            pltpu.VMEM((zs * ants, ants * in_band), jnp.bfloat16),
            dma((zs - 1,)),
            dma((zs - 1,)),
            dma(()),
            dma(()),
            dma(()),
            dma(()),
            dma((steps, CUTS)),
            dma((steps, CUTS)),
        ],
        compiler_params=pltpu.CompilerParams(
            collective_id=0, has_side_effects=True, vmem_limit_bytes=48 * 1024 * 1024
        ),
    )(
        chan_order, delays.reshape(rounds, total), lines, gain, pos, directions, antenna_row_lookup.reshape(1, antennas)
    )
    return out.reshape(1, 2, bins, half)


def solution(mesh):
    placed = (
        P(None, "chan", "band", None, "group"),
        P(None, "band", "chan", None),
        P(),
        P(None, ("group", "beam")),
        P(),
        P(),
        P(),
    )
    return jax.shard_map(
        shards,
        mesh=mesh,
        in_specs=placed,
        out_specs=P("band", "chan", None, ("group", "beam")),
        check_vma=False,
    )
```

time: 94.5 us -> 49.3 us (0.52)
  Pallas kernels: 0 us -> 43 us
  other arithmetic: 38.1 us -> 0 us
  waiting for transfers between devices: 22.3 us -> 0 us
  local copies, waits for them, and re-layouts: 20 us -> 5.82 us
  starting transfers between devices: 8.15 us -> 0 us
  matrix products: 5.44 us -> 0 us
    pallas_call x0 -> x1, Pallas kernels: none -> 43 us  [shards(): pl.pallas_call(functools.partial(kernel, zs, bands, total), out_shape=jax...]
    neg x1 -> x0, other arithmetic: 16.1 us -> none  [beam_weights(): lower_rows = jnp.concatenate([-w_im, w_re], axis=2)]
    convert_element_type x1 -> x0, other arithmetic: 15.9 us -> none  [beam_weights(): w_re = ((g_re * cosine + g_im * sine) * factor).astype(jnp.bfloat16)]
    ppermute x3 -> x0, waiting for transfers between devices: 14.6 us -> none  [partner_2(): return lax.ppermute(value, axis, pairs)]
    all_to_all x1 -> x0, waiting for transfers between devices: 7.65 us -> none  [shards(): lax.all_to_all(voltages, 'chan', split_axis=3, concat_axis=1, tiled=True)]
    gather x5 -> x0, local copies, waits for them, and re-layouts: 7.11 us -> none  [the longest x4 4.3 us: one_row(): return lax.dynamic_slice_in_dim(row, length - shift, length, 0)]
    all_to_all x1 -> x0, starting transfers between devices: 6.45 us -> none  [shards(): lax.all_to_all(voltages, 'chan', split_axis=3, concat_axis=1, tiled=True)]
    dot_general x1 -> x0, matrix products: 5.44 us -> none  [shards(): jnp.einsum('pacn,cpaq->cnq', flat, weights, preferred_element_type=jnp.fl...]
  transfers between devices with their start and end apart: 4 -> 0, of which waited for: 4 -> 0; matrix products, arithmetic and copies ran while one was open for 43% -> 0% of each run, Pallas kernels for 0% -> 0%
where the time goes in v1:
time: 49.3 us; the launch traced here: 48.9 us
  Pallas kernels  43 us (87%)
  local copies, waits for them, and re-layouts  5.82 us (12%)
    pallas_call x1, Pallas kernels, shards(): pl.pallas_call(functools.partial(kernel, zs, bands, total), out_shape=jax...  43 us
    unnamed x12, local copies, waits for them, and re-layouts  4.3 us

profile of v1, /device:TPU:0, one launch (start us, length us, event | category | flops | bytes accessed | tf_op | source)
XLA Modules:
  0.0 48.9 jit_solution(1446018596979920516)
XLA Ops:
  0.0 0.0 copy-start
  0.0 0.8 %reshape.14.delay_ref = s32[4,16]{1,0:T(4,128)S(1)} reshape(s32[4,2,8]{2,1,0:T(2,128)} %param.13) | data formatting | bytes 512 | tf_op jit(solution)/shard_map/reshape | solution.py:262
  0.8 0.0 copy-done
  0.8 0.7 %pad.9.pos_ref = f32[8,1024]{1,0:T(8,128)S(1)} pad(f32[3,1024]{1,0:T(4,128)} %param.9, f32[]{:T(128)} %constant.13.clone.1), padding=0_5x0_0 | pad | bytes 45060 | tf_op jit(solution)/shard_map/jit(_pad)/pad | solution.py:228
  1.6 0.0 copy-start.1
  1.6 1.6 %copy-done.1 = bf16[2,256,1,8,256]{4,3,2,1,0:T(8,128)(2,1)S(1)} copy-done((bf16[2,256,1,8,256]{4,3,2,1,0:T(8,128)(2,1)S(1)}, bf16[2,256,1,8,256]{4,3,2,1,0:T(8,128)(2,1)}, u32[]{:S(2)}) %copy-start.1) | copy-done | bytes 2097176
  3.2 0.0 copy-start.2
  3.2 0.7 %copy-done.2 = f32[3,512]{1,0:T(4,128)S(1)} copy-done((f32[3,512]{1,0:T(4,128)S(1)}, f32[3,512]{1,0:T(4,128)}, u32[]{:S(2)}) %copy-start.2) | copy-done | bytes 6168
  3.8 0.0 copy-start.3
  3.9 0.7 %copy-done.3 = s32[1024]{0:T(1024)S(1)} copy-done((s32[1024]{0:T(1024)S(1)}, s32[1024]{0:T(1024)}, u32[]{:S(2)}) %copy-start.3) | copy-done | bytes 4120
  4.5 0.0 copy-start.4
  4.5 0.7 %copy-done.4 = s32[16]{0:T(128)S(1)} copy-done((s32[16]{0:T(128)S(1)}, s32[16]{0:T(128)}, u32[]{:S(2)}) %copy-start.4) | copy-done | bytes 88
  5.2 43.0 %shard_map.73 = f32[2,32,512]{2,1,0:T(8,128)S(1)} custom-call(s32[16]{0:T(128)S(1)} %copy-done.4, s32[4,16]{1,0:T(4,128)S(1)} %reshape.14.delay_ref, bf16[2,2048,256]{2,1,0:T(8,128)(2,1)S(1)} %bitcast.6, f32[8,1024]{1,0:T(8,128)S(1)} %pad.8.gain_ref, f32[8,1024]{1,0:T(8,128)S(1)} %pad.9.pos_ref, f32[3,512]{1,0:T(4,128)S(1)} %copy-done.2, s32[1,1024]{1,0:T(1,128)S(1)} %bitcast.8), custom_call_target="tpu_custom_call" | custom-call | tf_op jit(solution)/shard_map/pallas_call | solution.py:232
  48.2 0.7 %copy.12 = f32[1,2,32,512]{3,2,1,0:T(8,128)} copy(f32[1,2,32,512]{3,2,1,0:T(8,128)S(1)} %bitcast.7) | data formatting | bytes 262144
  (3 shorter events, 0.0 us)
Async XLA Ops:
  0.0 0.8 %copy-start = (f32[2,1,2,1024]{3,2,1,0:T(2,128)S(1)}, f32[2,1,2,1024]{3,2,1,0:T(2,128)}, u32[]{:S(2)}) copy-start(f32[2,1,2,1024]{3,2,1,0:T(2,128)} %param.8) | copy-start | bytes 49156
  1.6 1.6 %copy-start.1 = (bf16[2,256,1,8,256]{4,3,2,1,0:T(8,128)(2,1)S(1)}, bf16[2,256,1,8,256]{4,3,2,1,0:T(8,128)(2,1)}, u32[]{:S(2)}) copy-start(bf16[2,256,1,8,256]{4,3,2,1,0:T(8,128)(2,1)} %param.7) | copy-start | bytes 6291460
  3.2 0.7 %copy-start.2 = (f32[3,512]{1,0:T(4,128)S(1)}, f32[3,512]{1,0:T(4,128)}, u32[]{:S(2)}) copy-start(f32[3,512]{1,0:T(4,128)} %dirs_ref.1) | copy-start | bytes 18436
  3.8 0.7 %copy-start.3 = (s32[1024]{0:T(1024)S(1)}, s32[1024]{0:T(1024)}, u32[]{:S(2)}) copy-start(s32[1024]{0:T(1024)} %param.11) | copy-start | bytes 12292
  4.5 0.7 %copy-start.4 = (s32[16]{0:T(128)S(1)}, s32[16]{0:T(128)}, u32[]{:S(2)}) copy-start(s32[16]{0:T(128)} %order_ref.1) | copy-start | bytes 196

commit v2 on v1

v2 whole, which is shorter than its diff:
```python
import functools
import math

import jax
import jax.numpy as jnp
from jax import lax
from jax.experimental import pallas as pl
from jax.experimental.pallas import tpu as pltpu
from jax.sharding import PartitionSpec as P

INTEG = 8
MESH = pl.DeviceIdType.MESH
SIN = (4.44288283, -7.30824114, 3.60628867, -0.84576206, 0.10920298)
COS = (1.4142135, -6.97885095, 5.73946031, -1.88355744, 0.31068696)


def horner(coefs, x):
    total = jnp.full_like(x, coefs[-1])
    for coef in coefs[-2::-1]:
        total = total * x + coef
    return total


def roll_down(state, shift):
    rows = state.shape[0]
    for bit in range(rows.bit_length() - 1):
        moved = pltpu.roll(state, 1 << bit, 0)
        state = jnp.where((shift >> bit) & 1 == 1, moved, state)
    return state


def kernel(
    zs, bands, total, order_in, delay_in, volt_in, gain_in, pos_in, dirs_in, lookup_in, out_ref,
    order_ref, delay_ref, volt_ref, gain_ref, pos_ref, dirs_ref, lookup_ref,
    send, recv, lines, table, weights, acc, other_dirs, tx, state, fin_tx, fin_rx, rx, select,
    load, v_send, v_recv, d_send, d_recv, l_send, l_recv, f_send, f_recv,
):
    z = lax.axis_index("chan")
    x = lax.axis_index("band")
    core = lax.axis_index("beam")
    antennas = lookup_ref.shape[1]
    local_ants = antennas // zs
    in_band = 2 * zs
    half = dirs_ref.shape[1]
    bins, chunk = rx.shape[1:]
    slot = x * in_band + z * 2 + core
    peers = [(h, dz, dx) for dx in range(bands) for dz in range(zs) for h in range(2)][1:]

    def at(h, dz, dx):
        return {"beam": core if h == 0 else 1 - core, "chan": (z + dz) % zs, "band": (x + dx) % bands}

    loads = [
        pltpu.make_async_copy(src, dst, load.at[no])
        for no, (src, dst) in enumerate(
            (
                (volt_in.at[0], volt_ref.at[0]), (volt_in.at[1], volt_ref.at[1]), (dirs_in, dirs_ref),
                (lookup_in, lookup_ref), (pos_in, pos_ref), (gain_in, gain_ref), (order_in, order_ref),
                (delay_in, delay_ref),
            )
        )
    ]
    for copy in loads:
        copy.start()
    barrier = pltpu.get_barrier_semaphore()
    for peer in peers:
        pl.semaphore_signal(barrier, inc=1, device_id=at(*peer), device_id_type=MESH)

    ants = select.shape[0] // zs
    rows = lax.broadcasted_iota(jnp.int32, select.shape, 0)
    cols = lax.broadcasted_iota(jnp.int32, select.shape, 1)
    ant_bits = ants.bit_length() - 1
    wanted = (rows & (ants - 1)) * in_band + (rows >> ant_bits) * 2 + core
    select[...] = jnp.where(cols == wanted, 1.0, 0.0).astype(jnp.bfloat16)
    copies = {}
    for part in range(2):
        loads[part].wait()
        for block in range(local_ants // ants):
            rows_in = volt_ref[part, block * ants * in_band : (block + 1) * ants * in_band, :]
            picked = jnp.dot(select[...], rows_in, preferred_element_type=jnp.float32).astype(jnp.bfloat16)
            start = part * local_ants + block * ants
            for dest in range(zs):
                send[dest, start : start + ants, :] = picked[dest * ants : (dest + 1) * ants]
        if part == 0:
            pl.semaphore_wait(barrier, len(peers))
        span = slice(part * local_ants, (part + 1) * local_ants)
        for d in range(1, zs):
            dest = (z + d) % zs
            copies[d, part] = pltpu.make_async_remote_copy(
                src_ref=send.at[dest, span], dst_ref=recv.at[d - 1, span],
                send_sem=v_send.at[d - 1, part], recv_sem=v_recv.at[d - 1, part],
                device_id=at(0, d, 0), device_id_type=MESH,
            )
            copies[d, part].start()
    loads[2].wait()
    dirs_copy = pltpu.make_async_remote_copy(
        src_ref=dirs_ref, dst_ref=other_dirs, send_sem=d_send, recv_sem=d_recv,
        device_id=at(1, 0, 0), device_id_type=MESH,
    )
    dirs_copy.start()
    for copy in loads[3:]:
        copy.wait()

    freq = 1.0 + order_ref[slot].astype(jnp.float32) / total
    lines[...] = jnp.zeros_like(lines)
    lines[0:3, :] = pos_ref[...]
    pos = lines[...]
    top = pos.astype(jnp.bfloat16)
    rest = pos - top.astype(jnp.float32)
    middle = rest.astype(jnp.bfloat16)
    last = (rest - middle.astype(jnp.float32)).astype(jnp.bfloat16)
    wide = 256
    for block in range(antennas // wide):
        span = slice(block * wide, (block + 1) * wide)
        row_no = lax.broadcasted_iota(jnp.int32, (antennas, wide), 0)
        hot = jnp.where(row_no == lookup_ref[:, span], 1.0, 0.0).astype(jnp.bfloat16)
        gathered = jnp.dot(top, hot, preferred_element_type=jnp.float32)
        gathered = gathered + jnp.dot(middle, hot, preferred_element_type=jnp.float32)
        gathered = gathered + jnp.dot(last, hot, preferred_element_type=jnp.float32)
        lines[0:3, span] = gathered[0:3] * freq
        for part in range(2):
            own = jnp.where(core == 0, gain_ref[part, 0, 0:1, span], gain_ref[part, 0, 1:2, span])
            lines[3 + part : 4 + part, span] = own * (1.0 / math.sqrt(antennas))
        table[span, :] = lines[:, span].T

    tile = 16

    def fill(side, dirs):
        def step(index, carry):
            d = index // (local_ants // tile)
            row = (index % (local_ants // tile)) * tile
            source = (z - d + zs) % zs
            info = table[pl.ds(pl.multiple_of(source * local_ants + row, tile), tile), :]
            turns = info[:, 0:1] * dirs[0:1, :] + info[:, 1:2] * dirs[1:2, :] + info[:, 2:3] * dirs[2:3, :]
            r = turns - lax.round(turns, lax.RoundingMethod.TO_NEAREST_EVEN)
            sq = r * r
            s = r * horner(SIN, sq)
            c = horner(COS, sq)
            sine = s * c
            cosine = 1.0 - s * s
            g_re, g_im = info[:, 3:4], info[:, 4:5]
            w_re = (g_re * cosine + g_im * sine).astype(jnp.bfloat16)
            w_im = (g_im * cosine - g_re * sine).astype(jnp.bfloat16)
            columns = slice(side * half, (side + 1) * half)
            first = pl.multiple_of(row, tile)
            weights[d, pl.ds(first, tile), columns] = w_im
            weights[d, pl.ds(local_ants + first, tile), columns] = w_re
            weights[d, pl.ds(2 * local_ants + first, tile), columns] = -w_im
            return carry

        lax.fori_loop(0, antennas // tile, step, 0, unroll=2)

    fill(0, dirs_ref)
    dirs_copy.wait()
    fill(1, other_dirs)

    contract = (((0,), (0,)), ((), ()))
    for d in range(zs):
        if d == 0:
            block = send[z]
        else:
            copies[d, 0].wait()
            copies[d, 1].wait()
            block = recv[d - 1]
        re = lax.dot_general(
            block, weights[d, local_ants : 3 * local_ants, :], contract, preferred_element_type=jnp.float32
        )
        im = lax.dot_general(
            block, weights[d, : 2 * local_ants, :], contract, preferred_element_type=jnp.float32
        )
        if d == 0:
            acc[0], acc[1] = re, im
        elif d < zs - 1:
            acc[0] += re
            acc[1] += im
        else:
            re = acc[0] + re
            im = acc[1] + im
    power = re * re + im * im
    binned = jnp.mean(power.reshape(bins, INTEG, 2 * half), axis=1)
    centred = (binned - jnp.mean(binned, axis=0, keepdims=True)) * (1.0 / math.sqrt(total))
    for h in range(2):
        for place in range(zs):
            start = h * half + place * chunk
            tx[h, place] = centred[:, start : start + chunk].astype(jnp.bfloat16)
    swaps = []
    for h, dz, dx in peers:
        copy = pltpu.make_async_remote_copy(
            src_ref=tx.at[h, (z + dz) % zs], dst_ref=rx.at[slot],
            send_sem=l_send.at[h, dz, dx], recv_sem=l_recv.at[h, dz, dx],
            device_id=at(h, dz, dx), device_id_type=MESH,
        )
        copy.start()
        swaps.append(copy)
    rx[slot] = tx[0, z]
    for copy in swaps:
        copy.wait()

    rounds = delay_ref.shape[0]

    def load_state(no, c):
        return rx[c].astype(jnp.float32) if no == 0 else state[no % 2, c]

    for no in range(rounds):
        stride = 1 << no

        def one(index, carry, no=no, stride=stride):
            c = index if no < rounds - 1 else x * in_band + index
            offset = (c // stride) % 2 * stride
            lower = load_state(no, c - offset)
            upper = load_state(no, c - offset + stride)
            shift = delay_ref[no, c // in_band, c % in_band]
            value = lower + roll_down(upper, shift)
            if no < rounds - 1:
                state[(no + 1) % 2, c] = value
            else:
                fin_tx[index // 2, index % 2] = value.astype(jnp.bfloat16)
            return carry

        count = total if no < rounds - 1 else in_band
        lax.fori_loop(0, count, one, 0, unroll=8)

    ends = []
    for d in range(1, zs):
        copy = pltpu.make_async_remote_copy(
            src_ref=fin_tx.at[(z + d) % zs], dst_ref=fin_rx.at[z], send_sem=f_send.at[d - 1],
            recv_sem=f_recv.at[d - 1], device_id=at(0, d, 0), device_id_type=MESH,
        )
        copy.start()
        ends.append(copy)
    fin_rx[z] = fin_tx[z]
    for copy in ends:
        copy.wait()
    for ch in range(2):
        parts = [fin_rx[source, ch].astype(jnp.float32) for source in range(zs)]
        out_ref[ch] = jnp.concatenate(parts, axis=1)


def shards(voltages, gains, positions, directions, antenna_row_lookup, chan_order, delays):
    zs = lax.axis_size("chan")
    bands = lax.axis_size("band")
    in_band = voltages.shape[3]
    total = in_band * bands
    antennas = positions.shape[1]
    local_ants = voltages.shape[1]
    samples = voltages.shape[4]
    bins = samples // INTEG
    half = directions.shape[1]
    ants = max(16, 256 // in_band)
    rounds = delays.shape[0]
    chunk = half // zs
    bf16, f32 = jnp.bfloat16, jnp.float32
    lines = voltages.reshape(2, local_ants * in_band, samples)
    lookup = antenna_row_lookup.reshape(1, antennas)
    dma = pltpu.SemaphoreType.DMA
    vmem = pltpu.VMEM
    out = pl.pallas_call(
        functools.partial(kernel, zs, bands, total),
        out_shape=jax.ShapeDtypeStruct((2, bins, half), f32),
        in_specs=[pl.BlockSpec(memory_space=pltpu.MemorySpace.HBM)] * 7,
        out_specs=pl.BlockSpec(memory_space=vmem),
        scratch_shapes=[
            pltpu.SMEM(chan_order.shape, jnp.int32),
            pltpu.SMEM(delays.shape, jnp.int32),
            vmem(lines.shape, bf16),
            vmem(gains.shape, f32),
            vmem(positions.shape, f32),
            vmem(directions.shape, f32),
            vmem(lookup.shape, jnp.int32),
            vmem((zs, 2 * local_ants, samples), bf16),
            vmem((zs - 1, 2 * local_ants, samples), bf16),
            vmem((8, antennas), f32),
            vmem((antennas, 8), f32),
            vmem((zs, 3 * local_ants, 2 * half), bf16),
            vmem((2, samples, 2 * half), f32),
            vmem(directions.shape, f32),
            vmem((2, zs, bins, chunk), bf16),
            vmem((2, total, bins, chunk), f32),
            vmem((zs, 2, bins, chunk), bf16),
            vmem((zs, 2, bins, chunk), bf16),
            vmem((total, bins, chunk), bf16),
            vmem((zs * ants, ants * in_band), bf16),
            dma((8,)),
            dma((zs - 1, 2)),
            dma((zs - 1, 2)),
            dma(()),
            dma(()),
            dma((2, zs, bands)),
            dma((2, zs, bands)),
            dma((zs - 1,)),
            dma((zs - 1,)),
        ],
        compiler_params=pltpu.CompilerParams(
            collective_id=0, has_side_effects=True, vmem_limit_bytes=56 * 1024 * 1024
        ),
    )(chan_order, delays, lines, gains, positions, directions, lookup)
    return out.reshape(1, 2, bins, half)


def solution(mesh):
    placed = (
        P(None, "chan", "band", None, "group"),
        P(None, "band", "chan", None),
        P(),
        P(None, ("group", "beam")),
        P(),
        P(),
        P(),
    )
    return jax.shard_map(
        shards,
        mesh=mesh,
        in_specs=placed,
        out_specs=P("band", "chan", None, ("group", "beam")),
        check_vma=False,
    )
```

time: 49.3 us -> 42.7 us (0.87)
  local copies, waits for them, and re-layouts: 5.82 us -> 1.57 us
  Pallas kernels: 43 us -> 40.9 us
    unnamed x12 -> x1, local copies, waits for them, and re-layouts: 4.3 us -> 1.57 us
    pallas_call x1, Pallas kernels: 43 us -> 40.9 us  [shards(): pl.pallas_call(functools.partial(kernel, zs, bands, total), out_shape=jax...]
    reshape x1 -> x0, local copies, waits for them, and re-layouts: 0.78 us -> none  [shards(): delays.reshape(rounds, total)]
    pad x2 -> x0, local copies, waits for them, and re-layouts: 0.74 us -> none  [the longest x1 0.73 us: shards(): pos = jnp.pad(positions, ((0, 5), (0, 0)))]
where the time goes in v2:
time: 42.7 us; the launch traced here: 42.5 us
  Pallas kernels  40.9 us (96%)
  local copies, waits for them, and re-layouts  1.57 us (4%)
    pallas_call x1, Pallas kernels, shards(): pl.pallas_call(functools.partial(kernel, zs, bands, total), out_shape=jax...  40.9 us
    unnamed x1, local copies, waits for them, and re-layouts  1.57 us

profile of v2, /device:TPU:0, one launch (start us, length us, event | category | flops | bytes accessed | tf_op | source)
XLA Modules:
  0.0 42.5 jit_solution(14363341408103849408)
XLA Ops:
  0.0 40.9 %shard_map.73 = f32[2,32,512]{2,1,0:T(8,128)} custom-call(s32[16]{0:T(128)} %order_in.1, s32[4,2,8]{2,1,0:T(2,128)} %delay_in.1, bf16[2,2048,256]{2,1,0:T(8,128)(2,1)} %bitcast.3, f32[2,1,2,1024]{3,2,1,0:T(2,128)} %gain_in.1, f32[3,1024]{1,0:T(4,128)} %pos_in.1, f32[3,512]{1,0:T(4,128)} %dirs_in.1, s32[1,1024]{1,0:T(1,128)} %bitcast.5), custom_call_target="tpu_custom_call" | custom-call | tf_op jit(solution)/shard_map/pallas_call | solution.py:256
  40.9 1.6 %copy.9 = f32[1,2,32,512]{3,2,1,0:T(8,128)} copy(f32[1,2,32,512]{3,2,1,0:T(8,128)} %bitcast.4) | data formatting | bytes 262144

commit v3 on v2

--- a/solution.py
+++ b/solution.py
@@ -29,8 +29,18 @@
     return state
 
 
+def pack(value, folds):
+    rows = value.shape[0] // folds
+    return jnp.concatenate([value[k * rows : (k + 1) * rows] for k in range(folds)], axis=1)
+
+
+def unpack(value, folds):
+    lanes = value.shape[1] // folds
+    return jnp.concatenate([value[:, k * lanes : (k + 1) * lanes] for k in range(folds)], axis=0)
+
+
 def kernel(
-    zs, bands, total, order_in, delay_in, volt_in, gain_in, pos_in, dirs_in, lookup_in, out_ref,
+    zs, bands, total, cuts, folds, order_in, delay_in, volt_in, gain_in, pos_in, dirs_in, lookup_in, out_ref,
     order_ref, delay_ref, volt_ref, gain_ref, pos_ref, dirs_ref, lookup_ref,
     send, recv, lines, table, weights, acc, other_dirs, tx, state, fin_tx, fin_rx, rx, select,
     load, v_send, v_recv, d_send, d_recv, l_send, l_recv, f_send, f_recv,
@@ -42,7 +52,9 @@
     local_ants = antennas // zs
     in_band = 2 * zs
     half = dirs_ref.shape[1]
-    bins, chunk = rx.shape[1:]
+    bins, chunk = state.shape[2:]
+    order = [zs // 2] + [d for d in range(1, zs) if d != zs // 2]
+    spot = z * cuts + (x if cuts > 1 else 0)
     slot = x * in_band + z * 2 + core
     peers = [(h, dz, dx) for dx in range(bands) for dz in range(zs) for h in range(2)][1:]
 
@@ -83,7 +95,7 @@
         if part == 0:
             pl.semaphore_wait(barrier, len(peers))
         span = slice(part * local_ants, (part + 1) * local_ants)
-        for d in range(1, zs):
+        for d in order:
             dest = (z + d) % zs
             copies[d, part] = pltpu.make_async_remote_copy(
                 src_ref=send.at[dest, span], dst_ref=recv.at[d - 1, span],
@@ -147,14 +159,14 @@
             weights[d, pl.ds(2 * local_ants + first, tile), columns] = -w_im
             return carry
 
-        lax.fori_loop(0, antennas // tile, step, 0, unroll=2)
+        lax.fori_loop(0, antennas // tile, step, 0, unroll=4)
 
     fill(0, dirs_ref)
     dirs_copy.wait()
     fill(1, other_dirs)
 
     contract = (((0,), (0,)), ((), ()))
-    for d in range(zs):
+    for d in [0] + order:
         if d == 0:
             block = send[z]
         else:
@@ -169,7 +181,7 @@
         )
         if d == 0:
             acc[0], acc[1] = re, im
-        elif d < zs - 1:
+        elif d != order[-1]:
             acc[0] += re
             acc[1] += im
         else:
@@ -179,59 +191,66 @@
     binned = jnp.mean(power.reshape(bins, INTEG, 2 * half), axis=1)
     centred = (binned - jnp.mean(binned, axis=0, keepdims=True)) * (1.0 / math.sqrt(total))
     for h in range(2):
-        for place in range(zs):
+        for place in range(zs * cuts):
             start = h * half + place * chunk
-            tx[h, place] = centred[:, start : start + chunk].astype(jnp.bfloat16)
+            tx[h, place] = pack(centred[:, start : start + chunk], folds).astype(jnp.bfloat16)
     swaps = []
-    for h, dz, dx in peers:
-        copy = pltpu.make_async_remote_copy(
-            src_ref=tx.at[h, (z + dz) % zs], dst_ref=rx.at[slot],
-            send_sem=l_send.at[h, dz, dx], recv_sem=l_recv.at[h, dz, dx],
-            device_id=at(h, dz, dx), device_id_type=MESH,
-        )
-        copy.start()
-        swaps.append(copy)
-    rx[slot] = tx[0, z]
+    for dz in order + [0]:
+        for dx in range(bands):
+            for h in range(2):
+                if (h, dz, dx) == (0, 0, 0):
+                    continue
+                place = (z + dz) % zs * cuts + ((x + dx) % bands if cuts > 1 else 0)
+                copy = pltpu.make_async_remote_copy(
+                    src_ref=tx.at[h, place], dst_ref=rx.at[slot],
+                    send_sem=l_send.at[h, dz, dx], recv_sem=l_recv.at[h, dz, dx],
+                    device_id=at(h, dz, dx), device_id_type=MESH,
+                )
+                copy.start()
+                swaps.append(copy)
+    rx[slot] = tx[0, spot]
     for copy in swaps:
         copy.wait()
 
     rounds = delay_ref.shape[0]
 
     def load_state(no, c):
-        return rx[c].astype(jnp.float32) if no == 0 else state[no % 2, c]
-
-    for no in range(rounds):
+        return unpack(rx[c].astype(jnp.float32), folds) if no == 0 else state[no % 2, c]
+
+    def merged(no, c):
         stride = 1 << no
-
-        def one(index, carry, no=no, stride=stride):
-            c = index if no < rounds - 1 else x * in_band + index
-            offset = (c // stride) % 2 * stride
-            lower = load_state(no, c - offset)
-            upper = load_state(no, c - offset + stride)
-            shift = delay_ref[no, c // in_band, c % in_band]
-            value = lower + roll_down(upper, shift)
-            if no < rounds - 1:
-                state[(no + 1) % 2, c] = value
-            else:
-                fin_tx[index // 2, index % 2] = value.astype(jnp.bfloat16)
+        offset = (c // stride) % 2 * stride
+        lower = load_state(no, c - offset)
+        upper = load_state(no, c - offset + stride)
+        return lower + roll_down(upper, delay_ref[no, c // in_band, c % in_band])
+
+    for no in range(rounds - 1):
+
+        def one(c, carry, no=no):
+            state[(no + 1) % 2, c] = merged(no, c)
             return carry
 
-        count = total if no < rounds - 1 else in_band
-        lax.fori_loop(0, count, one, 0, unroll=8)
+        lax.fori_loop(0, total, one, 0, unroll=16)
 
     ends = []
-    for d in range(1, zs):
-        copy = pltpu.make_async_remote_copy(
-            src_ref=fin_tx.at[(z + d) % zs], dst_ref=fin_rx.at[z], send_sem=f_send.at[d - 1],
-            recv_sem=f_recv.at[d - 1], device_id=at(0, d, 0), device_id_type=MESH,
-        )
-        copy.start()
-        ends.append(copy)
-    fin_rx[z] = fin_tx[z]
+    for dz, dx in [(dz, dx) for dz in order + [0] for dx in range(cuts)]:
+        to_z, to_x = (z + dz) % zs, (x + dx) % bands
+        place = to_z * cuts + (to_x if cuts > 1 else 0)
+        for ch in range(2):
+            value = merged(rounds - 1, to_x * in_band + 2 * to_z + ch)
+            fin_tx[place, ch] = pack(value, folds).astype(jnp.bfloat16)
+        if (dz, dx) != (0, 0):
+            copy = pltpu.make_async_remote_copy(
+                src_ref=fin_tx.at[place], dst_ref=fin_rx.at[spot], send_sem=f_send.at[dz, dx],
+                recv_sem=f_recv.at[dz, dx], device_id=at(0, dz, dx), device_id_type=MESH,
+            )
+            copy.start()
+            ends.append(copy)
+    fin_rx[spot] = fin_tx[spot]
     for copy in ends:
         copy.wait()
     for ch in range(2):
-        parts = [fin_rx[source, ch].astype(jnp.float32) for source in range(zs)]
+        parts = [unpack(fin_rx[source, ch].astype(jnp.float32), folds) for source in range(zs * cuts)]
         out_ref[ch] = jnp.concatenate(parts, axis=1)
 
 
@@ -247,14 +266,17 @@
     half = directions.shape[1]
     ants = max(16, 256 // in_band)
     rounds = delays.shape[0]
-    chunk = half // zs
+    cuts = 1
+    chunk = half // (zs * cuts)
+    folds = 2 if 2 * chunk == 128 else 1
+    packed = (bins // folds, chunk * folds)
     bf16, f32 = jnp.bfloat16, jnp.float32
     lines = voltages.reshape(2, local_ants * in_band, samples)
     lookup = antenna_row_lookup.reshape(1, antennas)
     dma = pltpu.SemaphoreType.DMA
     vmem = pltpu.VMEM
     out = pl.pallas_call(
-        functools.partial(kernel, zs, bands, total),
+        functools.partial(kernel, zs, bands, total, cuts, folds),
         out_shape=jax.ShapeDtypeStruct((2, bins, half), f32),
         in_specs=[pl.BlockSpec(memory_space=pltpu.MemorySpace.HBM)] * 7,
         out_specs=pl.BlockSpec(memory_space=vmem),
@@ -273,11 +295,11 @@
             vmem((zs, 3 * local_ants, 2 * half), bf16),
             vmem((2, samples, 2 * half), f32),
             vmem(directions.shape, f32),
-            vmem((2, zs, bins, chunk), bf16),
+            vmem((2, zs * cuts, *packed), bf16),
             vmem((2, total, bins, chunk), f32),
-            vmem((zs, 2, bins, chunk), bf16),
-            vmem((zs, 2, bins, chunk), bf16),
-            vmem((total, bins, chunk), bf16),
+            vmem((zs * cuts, 2, *packed), bf16),
+            vmem((zs * cuts, 2, *packed), bf16),
+            vmem((total, *packed), bf16),
             vmem((zs * ants, ants * in_band), bf16),
             dma((8,)),
             dma((zs - 1, 2)),
@@ -286,8 +308,8 @@
             dma(()),
             dma((2, zs, bands)),
             dma((2, zs, bands)),
-            dma((zs - 1,)),
-            dma((zs - 1,)),
+            dma((zs, cuts)),
+            dma((zs, cuts)),
         ],
         compiler_params=pltpu.CompilerParams(
             collective_id=0, has_side_effects=True, vmem_limit_bytes=56 * 1024 * 1024

time: 42.7 us -> 42.1 us (0.986)
  Pallas kernels: 40.9 us -> 40.3 us
    pallas_call x1, Pallas kernels: 40.9 us -> 40.3 us  [shards(): pl.pallas_call(functools.partial(kernel, zs, bands, total, cuts, folds),...]
where the time goes in v3:
time: 42.1 us; the launch traced here: 41.9 us
  Pallas kernels  40.3 us (96%)
  local copies, waits for them, and re-layouts  1.57 us (4%)
    pallas_call x1, Pallas kernels, shards(): pl.pallas_call(functools.partial(kernel, zs, bands, total, cuts, folds),...  40.3 us
    unnamed x1, local copies, waits for them, and re-layouts  1.57 us

profile of v3, /device:TPU:0, one launch (start us, length us, event | category | flops | bytes accessed | tf_op | source)
XLA Modules:
  0.0 41.9 jit_solution(9277646021439496251)
XLA Ops:
  0.0 40.3 %shard_map.73 = f32[2,32,512]{2,1,0:T(8,128)} custom-call(s32[16]{0:T(128)} %order_in.1, s32[4,2,8]{2,1,0:T(2,128)} %delay_in.1, bf16[2,2048,256]{2,1,0:T(8,128)(2,1)} %bitcast.3, f32[2,1,2,1024]{3,2,1,0:T(2,128)} %gain_in.1, f32[3,1024]{1,0:T(4,128)} %pos_in.1, f32[3,512]{1,0:T(4,128)} %dirs_in.1, s32[1,1024]{1,0:T(1,128)} %bitcast.5), custom_call_target="tpu_custom_call" | custom-call | tf_op jit(solution)/shard_map/pallas_call | solution.py:278
  40.3 1.6 %copy.9 = f32[1,2,32,512]{3,2,1,0:T(8,128)} copy(f32[1,2,32,512]{3,2,1,0:T(8,128)} %bitcast.4) | data formatting | bytes 262144

commit v4 on v3

--- a/solution.py
+++ b/solution.py
@@ -170,8 +170,8 @@
         if d == 0:
             block = send[z]
         else:
-            copies[d, 0].wait()
-            copies[d, 1].wait()
+            copies[d, 0].wait_recv()
+            copies[d, 1].wait_recv()
             block = recv[d - 1]
         re = lax.dot_general(
             block, weights[d, local_ants : 3 * local_ants, :], contract, preferred_element_type=jnp.float32
@@ -210,7 +210,7 @@
                 swaps.append(copy)
     rx[slot] = tx[0, spot]
     for copy in swaps:
-        copy.wait()
+        copy.wait_recv()
 
     rounds = delay_ref.shape[0]
 
@@ -248,10 +248,12 @@
             ends.append(copy)
     fin_rx[spot] = fin_tx[spot]
     for copy in ends:
-        copy.wait()
+        copy.wait_recv()
     for ch in range(2):
         parts = [unpack(fin_rx[source, ch].astype(jnp.float32), folds) for source in range(zs * cuts)]
         out_ref[ch] = jnp.concatenate(parts, axis=1)
+    for copy in [*copies.values(), *swaps, *ends]:
+        copy.wait_send()
 
 
 def shards(voltages, gains, positions, directions, antenna_row_lookup, chan_order, delays):

time: 42.1 us -> 42.1 us (level)
  no operation moved by 1% of the time
where the time goes in v4:
time: 42.1 us; the launch traced here: 41.9 us
  Pallas kernels  40.4 us (96%)
  local copies, waits for them, and re-layouts  1.57 us (4%)
    pallas_call x1, Pallas kernels, shards(): pl.pallas_call(functools.partial(kernel, zs, bands, total, cuts, folds),...  40.4 us
    unnamed x1, local copies, waits for them, and re-layouts  1.57 us

profile of v4, /device:TPU:0, one launch (start us, length us, event | category | flops | bytes accessed | tf_op | source)
XLA Modules:
  0.0 41.9 jit_solution(7446965659213101680)
XLA Ops:
  0.0 40.4 %shard_map.73 = f32[2,32,512]{2,1,0:T(8,128)} custom-call(s32[16]{0:T(128)} %order_in.1, s32[4,2,8]{2,1,0:T(2,128)} %delay_in.1, bf16[2,2048,256]{2,1,0:T(8,128)(2,1)} %bitcast.3, f32[2,1,2,1024]{3,2,1,0:T(2,128)} %gain_in.1, f32[3,1024]{1,0:T(4,128)} %pos_in.1, f32[3,512]{1,0:T(4,128)} %dirs_in.1, s32[1,1024]{1,0:T(1,128)} %bitcast.5), custom_call_target="tpu_custom_call" | custom-call | tf_op jit(solution)/shard_map/pallas_call | solution.py:280
  40.4 1.6 %copy.9 = f32[1,2,32,512]{3,2,1,0:T(8,128)} copy(f32[1,2,32,512]{3,2,1,0:T(8,128)} %bitcast.4) | data formatting | bytes 262144
